TPU v7x, 256 devices: a whole 4x4x8 slice. The times are simulated.
256 devices in a mesh: occ: 64 (over z, y, core), ao: 4 (over x).
Axes of the slice: x: 4, y: 4, z: 8, core: 2. Of those that a mesh axis runs over, the one named last changes fastest.
Arguments:
- amplitudes: bfloat16 [256, 256, 256], P('occ', None, 'ao'), may hold values from -6 to 6
- orbitals: bfloat16 [512, 256], replicated, may hold values from -0.375 to 0.375
- tiles: bfloat16 [4096, 512, 512], P('occ', None, 'ao'), may hold values from -0.125 to 0.125
- tile_count: int32 [64], replicated, may hold values from 1 to 64, 2048 in all
- tile_row: int32 [4096], replicated, may hold values from 0 to 7
- tile_src: int32 [4096, 1], replicated, may hold values from 0 to 63; in each aligned block of 64 rows (0 to 63, 64 to 127, ...) at most 2 rows name the same one
- tile_sub: int32 [4096], replicated, may hold values from 0 to 7
Outputs:
- sigma_out: bfloat16 [256, 256, 256], P('occ', None, 'ao')
Inputs may be any that keep to these rules, and one draw needn't show every extreme that they name: `tile_count`: each occ index owns between 1 and 64 live slots, the first ones of its 64 slots; some index owns exactly 64. `tile_src`: among the 64 slots of one owner no source index is named more than 2 times, and some owner names one source exactly 2 times.
All inputs are finite; a program needn't handle non-finite values.
Results may differ from a plain program's by a relative error of at most 0.024.
Values may be sent and summed in bfloat16 or wider, within the bound.
A program may use at most 128 MiB of HBM per device.

v0:
```python
import jax
import jax.numpy as jnp
from jax import lax
from jax.sharding import PartitionSpec as P


def shards(amplitudes, orbitals, tiles, tile_count, tile_row, tile_src, tile_sub):
    node_count = lax.axis_size("occ")
    own_index = lax.axis_index("occ")
    quarter = lax.axis_index("ao")
    local_occ, vir_count, vir_part = amplitudes.shape
    ao_count = orbitals.shape[0]
    ao_part = ao_count // lax.axis_size("ao")
    slot_count = tiles.shape[0]
    blocks = ao_count // node_count
    nu_rows = lax.dynamic_slice_in_dim(orbitals, quarter * ao_part, ao_part, 0)
    vir_cols = lax.dynamic_slice_in_dim(orbitals, quarter * vir_part, vir_part, 1)
    partial_x = jnp.einsum("icd,nd->icn", amplitudes, vir_cols, preferred_element_type=jnp.float32)
    half_pairs = lax.psum_scatter(
        partial_x.astype(jnp.bfloat16), "ao", scatter_dimension=2, tiled=True
    )
    pair_rows = jnp.einsum(
        "mc,icn->imn", orbitals, half_pairs, preferred_element_type=jnp.float32
    ).astype(jnp.bfloat16)
    sources = tile_src[:, 0].reshape(node_count, slot_count)
    sub_blocks = tile_sub.reshape(node_count, slot_count)
    own_src = lax.dynamic_index_in_dim(sources, own_index, 0, keepdims=False)
    home_rows = lax.all_to_all(pair_rows, "occ", split_axis=1, concat_axis=0, tiled=True)
    per_peer = max(2, (slot_count + node_count - 1) // node_count)
    matches = sources == own_index
    send_rank = jnp.cumsum(matches.astype(jnp.int32), axis=1) - 1
    levels = jnp.arange(per_peer, dtype=jnp.int32)
    chosen = matches[:, None, :] & (send_rank[:, None, :] == levels[None, :, None])
    block_id = jnp.sum(jnp.where(chosen, sub_blocks[:, None, :], 0), axis=2)
    all_occ = home_rows.shape[0]
    packed = jnp.take(home_rows, block_id.reshape(-1), axis=1).reshape(
        all_occ, node_count, per_peer, ao_part
    )
    arrived = lax.all_to_all(packed, "occ", split_axis=1, concat_axis=1, tiled=True)
    positions = jnp.arange(slot_count, dtype=jnp.int32)
    earlier = positions[:, None] > positions[None, :]
    same_src = own_src[:, None] == own_src[None, :]
    own_rank = jnp.sum((earlier & same_src).astype(jnp.int32), axis=1)
    fetched = jnp.take(
        arrived.reshape(all_occ, node_count * per_peer, ao_part),
        own_src * per_peer + own_rank,
        axis=1,
    )
    live_mask = jnp.arange(slot_count, dtype=jnp.int32) < tile_count[own_index]
    own_row = lax.dynamic_index_in_dim(
        tile_row.reshape(node_count, slot_count), own_index, 0, keepdims=False
    )
    onehot = (
        (own_row[:, None] == jnp.arange(blocks, dtype=jnp.int32)[None, :]) & live_mask[:, None]
    ).astype(jnp.bfloat16)
    products = jnp.einsum("itn,tsn->tis", fetched, tiles, preferred_element_type=jnp.float32)
    upper_part = products.astype(jnp.bfloat16)
    lower_part = (products - upper_part.astype(jnp.float32)).astype(jnp.bfloat16)
    partial_z = jnp.einsum("tr,tis->irs", onehot, upper_part, preferred_element_type=jnp.float32)
    partial_z = partial_z + jnp.einsum(
        "tr,tis->irs", onehot, lower_part, preferred_element_type=jnp.float32
    )
    ladder = lax.psum_scatter(partial_z.astype(jnp.bfloat16), "ao", scatter_dimension=2, tiled=True)
    back_rows = lax.all_to_all(ladder, "occ", split_axis=0, concat_axis=1, tiled=True)
    mixed = jnp.einsum(
        "la,ils->ias", orbitals, back_rows, preferred_element_type=jnp.float32
    ).astype(jnp.bfloat16)
    partial_s = jnp.einsum("ias,sb->iab", mixed, nu_rows, preferred_element_type=jnp.float32)
    return lax.psum_scatter(partial_s.astype(jnp.bfloat16), "ao", scatter_dimension=2, tiled=True)


def solution(mesh):
    placed = (P("occ", None, "ao"), P(), P("occ", None, "ao"), P(), P(), P(), P())
    return jax.shard_map(
        shards, mesh=mesh, in_specs=placed, out_specs=P("occ", None, "ao"), check_vma=False
    )
```

profile of v0, /device:TPU:8, one launch (start us, length us, event | category | flops | bytes accessed | tf_op | source)
XLA Modules:
  0.0 509.5 jit_solution(4199454795965634853)
XLA Ops:
  7.5 2.4 fusion.12
  10.4 1.4 reduce.3
  11.9 27.3 %reduce-scatter.6.cloned.1.call-done = bf16[4,256,128]{1,2,0:T(8,128)(2,1)} async-done(((bf16[4,256,512]{1,2,0:T(8,128)(2,1)}), bf16[4,256,128]{1,2,0:T(8,128)(2,1)}) %reduce-scatter.6.cloned.1.call-update) | async-done | bytes 262160 | tf_op jit(solution)/shard_map/reduce_scatter | solution.py:19
  39.1 1.3 fusion.13
  40.4 1.1 copy.41
  41.5 10.6 %all-to-all-start = ((bf16[4,512,128]{2,0,1:T(4,128)(2,1)}), bf16[4,512,128]{2,0,1:T(4,128)(2,1)S(1)}, u32[]{:S(2)}, u32[]{:S(2)}) async-start(bf16[4,512,128]{2,0,1:T(4,128)(2,1)} %copy.41), calls=%async_computation.1 | async-start | bytes 1048576 | tf_op jit(solution)/shard_map/all_to_all | solution.py:28
  53.6 16.0 %all-to-all-done = bf16[4,512,128]{2,0,1:T(4,128)(2,1)S(1)} async-done(((bf16[4,512,128]{2,0,1:T(4,128)(2,1)}), bf16[4,512,128]{2,0,1:T(4,128)(2,1)S(1)}, u32[]{:S(2)}, u32[]{:S(2)}) %all-to-all-start) | async-done | bytes 524320 | tf_op jit(solution)/shard_map/all_to_all | solution.py:28
  69.8 6.4 %gather_fusion = bf16[128,256,128]{2,1,0:T(8,128)(2,1)} fusion(bf16[256,8,128]{2,0,1:T(8,128)(2,1)S(1)} %copy.45, s32[1024]{0:T(1024)S(1)} %pad_clamp_fusion.1), kind=kCustom, calls=%fused_computation | custom fusion | bytes 16777728 | tf_op jit(solution)/shard_map/jit(_take)/gather | solution.py:36
  76.2 7.4 %broadcast_select_fusion = bf16[256,64,2,128]{3,0,2,1:T(8,128)(2,1)} fusion(bf16[256,64,2,128]{3,0,2,1:T(8,128)(2,1)} %bitcast.74, pred[64,2]{1,0:T(8,128)(4,1)S(1)} %copy.39), kind=kLoop, calls=%fused_computation.7 | loop fusion | flops 4194304 | bytes 16777344 | tf_op jit(solution)/shard_map/jit(_take)/select_n | solution.py:36
  83.6 6.2 %all-to-all-start.1 = ((bf16[256,64,2,128]{3,0,2,1:T(8,128)(2,1)}), bf16[256,64,2,128]{3,0,2,1:T(8,128)(2,1)}, u32[]{:S(2)}, u32[]{:S(2)}) async-start(bf16[256,64,2,128]{3,0,2,1:T(8,128)(2,1)} %broadcast_select_fusion), calls=%async_computation.2 | async-start | bytes 16777216 | tf_op jit(solution)/shard_map/all_to_all | solution.py:39
  91.6 183.5 %all-to-all-done.1 = bf16[256,64,2,128]{3,0,2,1:T(8,128)(2,1)} async-done(((bf16[256,64,2,128]{3,0,2,1:T(8,128)(2,1)}), bf16[256,64,2,128]{3,0,2,1:T(8,128)(2,1)}, u32[]{:S(2)}, u32[]{:S(2)}) %all-to-all-start.1) | async-done | bytes 8388640 | tf_op jit(solution)/shard_map/all_to_all | solution.py:39
  275.1 6.5 %gather_fusion.1 = bf16[64,256,128]{2,1,0:T(8,128)(2,1)} fusion(bf16[256,128,128]{2,0,1:T(8,128)(2,1)} %bitcast.11, s32[1024]{0:T(1024)S(1)} %pad_clamp_fusion), kind=kCustom, calls=%fused_computation.1 | custom fusion | bytes 8388864 | tf_op jit(solution)/shard_map/jit(_take)/gather | solution.py:44
  281.6 19.5 %subtract_convert_fusion = (bf16[64,256,512]{2,1,0:T(8,128)(2,1)}, bf16[64,256,512]{2,1,0:T(8,128)(2,1)}) fusion(bf16[64,512,128]{2,1,0:T(8,128)(2,1)} %param.9, bf16[64,256,128]{2,1,0:T(8,128)(2,1)} %gather_fusion.1, pred[64]{0:T(512)(128)(4,1)S(1)} %compare_and_fusion.1), kind=kOutput, calls=%fused_computation.2 | convolution fusion | flops 2183135232 | bytes 46137408 | tf_op jit(solution)/shard_map/itn,tsn->tis/dot_general | solution.py:56
  301.1 16.7 %fusion = f32[256,512,8]{1,2,0:T(8,128)S(1)} fusion(bf16[64,256,512]{2,1,0:T(8,128)(2,1)} %get-tuple-element.5, s32[64]{0:T(128)S(1)} %fusion.38, pred[64]{0:T(512)(128)(4,1)S(1)} %iota_compare_fusion.3), kind=kOutput, calls=%fused_computation.3 | convolution fusion | flops 134218752 | bytes 20971840 | tf_op jit(solution)/shard_map/tr,tis->irs/dot_general | solution.py:60
  317.8 15.0 %fusion.8 = bf16[256,8,512]{2,1,0:T(8,128)(2,1)S(1)} fusion(f32[256,512,8]{1,2,0:T(8,128)S(1)} %fusion, bf16[64,256,512]{2,1,0:T(8,128)(2,1)} %get-tuple-element.6, s32[64]{0:T(128)S(1)} %fusion.38, pred[64]{0:T(512)(128)(4,1)S(1)} %iota_compare_fusion.3), kind=kOutput, calls=%fused_computation.13 | convolution fusion | flops 136315904 | bytes 23068992 | tf_op jit(solution)/shard_map/tr,tis->irs/dot_general | solution.py:59
  332.8 24.0 %copy.54 = bf16[256,8,512]{1,0,2:T(8,128)(2,1)} copy(bf16[256,8,512]{2,1,0:T(8,128)(2,1)S(1)} %fusion.8) | data formatting | bytes 4194304
  356.8 48.5 %reshape.130 = bf16[512,2048]{1,0:T(8,128)(2,1)} reshape(bf16[512,256,8]{2,1,0:T(8,128)(2,1)} %bitcast.73) | data formatting | bytes 4194304
  405.2 28.7 %reduce-scatter.10.cloned.1.call-done = bf16[128,2048]{1,0:T(8,128)(2,1)} async-done(((bf16[512,2048]{1,0:T(8,128)(2,1)}), bf16[128,2048]{1,0:T(8,128)(2,1)}) %reduce-scatter.10.cloned.1.call-update) | async-done | bytes 524304
  434.0 11.9 %reshape.131 = bf16[128,256,8]{2,1,0:T(8,128)(2,1)} reshape(bf16[128,2048]{1,0:T(8,128)(2,1)} %reduce-scatter.10.cloned.1.call-done) | data formatting | bytes 1048576
  445.8 8.2 %copy.55 = bf16[256,8,128]{2,1,0:T(8,128)(2,1)} copy(bf16[256,8,128]{1,0,2:T(8,128)(2,1)} %bitcast.75) | data formatting | bytes 1048576
  454.0 10.5 %all-to-all-start.2 = ((bf16[256,8,128]{2,1,0:T(8,128)(2,1)}), bf16[256,8,128]{2,1,0:T(8,128)(2,1)S(1)}, u32[]{:S(2)}, u32[]{:S(2)}) async-start(bf16[256,8,128]{2,1,0:T(8,128)(2,1)} %copy.55), calls=%async_computation.3 | async-start | bytes 1048576 | tf_op jit(solution)/shard_map/all_to_all | solution.py:64
  464.6 17.5 %all-to-all-done.2 = bf16[256,8,128]{2,1,0:T(8,128)(2,1)S(1)} async-done(((bf16[256,8,128]{2,1,0:T(8,128)(2,1)}), bf16[256,8,128]{2,1,0:T(8,128)(2,1)S(1)}, u32[]{:S(2)}, u32[]{:S(2)}) %all-to-all-start.2) | async-done | bytes 524320 | tf_op jit(solution)/shard_map/all_to_all | solution.py:64
  482.1 1.5 convolution_convert_fusion.2
  483.6 19.4 %reduce-scatter.8.cloned.1.call-done = bf16[4,256,64]{1,2,0:T(8,128)(2,1)} async-done(((bf16[4,256,256]{1,2,0:T(8,128)(2,1)}), bf16[4,256,64]{1,2,0:T(8,128)(2,1)}) %reduce-scatter.8.cloned.1.call-update) | async-done | bytes 131088 | tf_op jit(solution)/shard_map/reduce_scatter | solution.py:69
  (37 shorter events, 5.1 us)
Async XLA Ops:
  6.5 1.0 copy-start
  6.5 32.6 %reduce-scatter.6.cloned.1.call-start = ((), (), s32[]{:S(2)}) async-start(), calls=%async_computation.6 | async-start | bytes 1310720 | tf_op jit(solution)/shard_map/reduce_scatter | solution.py:19
  41.5 28.1 %all-to-all-start = ((bf16[4,512,128]{2,0,1:T(4,128)(2,1)}), bf16[4,512,128]{2,0,1:T(4,128)(2,1)S(1)}, u32[]{:S(2)}, u32[]{:S(2)}) async-start(bf16[4,512,128]{2,0,1:T(4,128)(2,1)} %copy.41), calls=%async_computation.1 | async-start | bytes 1048576 | tf_op jit(solution)/shard_map/all_to_all | solution.py:28
  83.6 6.4 %copy-start.1 = (s32[4096]{0:T(1024)S(1)}, s32[4096]{0:T(1024)}, u32[]{:S(2)}) copy-start(s32[4096]{0:T(1024)} %param.11) | copy-start | bytes 49156
  83.6 6.5 %copy-start.2 = (s32[64]{0:T(128)S(1)}, s32[64]{0:T(128)}, u32[]{:S(2)}) copy-start(s32[64]{0:T(128)} %param.10) | copy-start | bytes 772
  83.6 191.5 %all-to-all-start.1 = ((bf16[256,64,2,128]{3,0,2,1:T(8,128)(2,1)}), bf16[256,64,2,128]{3,0,2,1:T(8,128)(2,1)}, u32[]{:S(2)}, u32[]{:S(2)}) async-start(bf16[256,64,2,128]{3,0,2,1:T(8,128)(2,1)} %broadcast_select_fusion), calls=%async_computation.2 | async-start | bytes 16777216 | tf_op jit(solution)/shard_map/all_to_all | solution.py:39
  89.8 344.1 %reduce-scatter.10.cloned.1.call-start = ((), (), s32[]{:S(2)}) async-start(), calls=%async_computation.8 | async-start | bytes 2621440
  454.0 28.1 %all-to-all-start.2 = ((bf16[256,8,128]{2,1,0:T(8,128)(2,1)}), bf16[256,8,128]{2,1,0:T(8,128)(2,1)S(1)}, u32[]{:S(2)}, u32[]{:S(2)}) async-start(bf16[256,8,128]{2,1,0:T(8,128)(2,1)} %copy.55), calls=%async_computation.3 | async-start | bytes 1048576 | tf_op jit(solution)/shard_map/all_to_all | solution.py:64
  464.6 38.4 %reduce-scatter.8.cloned.1.call-start = ((), (), s32[]{:S(2)}) async-start(), calls=%async_computation.7 | async-start | bytes 655360 | tf_op jit(solution)/shard_map/reduce_scatter | solution.py:69
Sparse Core Ops, SparseCore 0:
  10.0 29.0 reduce-scatter.5
  405.4 28.5 reduce-scatter.9
  483.8 19.2 reduce-scatter.7
where the time goes:
time: 510 us
  waiting for transfers between devices  292 us (57%)
  local copies, waits for them, and re-layouts  110 us (22%)
  matrix products  56.3 us (11%)
  starting transfers between devices  27.5 us (5%)
  between operations  13.3 us (3%)
  other arithmetic  10 us (2%)
    all_to_all x1, waiting for transfers between devices, shards(): lax.all_to_all(packed, 'occ', split_axis=1, concat_axis=1, tiled=True)  183 us
    unnamed x11, local copies, waits for them, and re-layouts  93.9 us
    unnamed x4, waiting for transfers between devices  28.8 us
    reduce_scatter x1, waiting for transfers between devices, shards(): lax.psum_scatter(partial_x.astype(jnp.bfloat16), 'ao', scatter_dimension=...  27.3 us
    dot_general x1, matrix products, shards(): jnp.einsum('itn,tsn->tis', fetched, tiles, preferred_element_type=jnp.flo...  19.5 us
    reduce_scatter x1, waiting for transfers between devices, shards(): lax.psum_scatter(partial_s.astype(jnp.bfloat16), 'ao', scatter_dimension=...  19.4 us
    all_to_all x1, waiting for transfers between devices, shards(): lax.all_to_all(ladder, 'occ', split_axis=0, concat_axis=1, tiled=True)  17.5 us
    dot_general x1, matrix products, shards(): jnp.einsum('tr,tis->irs', onehot, lower_part, preferred_element_type=jnp....  16.7 us
  transfers between devices with their start and end apart: 6, of which 6 were waited for; matrix products, arithmetic and copies ran while one was open for 1% of the time, Pallas kernels for 0%

commit v1 on v0

--- a/solution.py
+++ b/solution.py
@@ -2,6 +2,12 @@
 import jax.numpy as jnp
 from jax import lax
 from jax.sharding import PartitionSpec as P
+
+
+def exchange_blocks(shard, name, split, join):
+    pieces = jnp.split(shard, lax.axis_size(name), axis=split)
+    received = lax.all_to_all(jnp.stack(pieces), name, 0, 0)
+    return jnp.concatenate(received, axis=join)
 
 
 def shards(amplitudes, orbitals, tiles, tile_count, tile_row, tile_src, tile_sub):
@@ -25,7 +31,7 @@
     sources = tile_src[:, 0].reshape(node_count, slot_count)
     sub_blocks = tile_sub.reshape(node_count, slot_count)
     own_src = lax.dynamic_index_in_dim(sources, own_index, 0, keepdims=False)
-    home_rows = lax.all_to_all(pair_rows, "occ", split_axis=1, concat_axis=0, tiled=True)
+    home_rows = exchange_blocks(pair_rows, "occ", 1, 0)
     per_peer = max(2, (slot_count + node_count - 1) // node_count)
     matches = sources == own_index
     send_rank = jnp.cumsum(matches.astype(jnp.int32), axis=1) - 1

time: 510 us -> 625 us (1.23); the launches traced: 510 us -> 615 us
  local copies, waits for them, and re-layouts: 110 us -> 218 us
    another operation x0 -> x69, local copies, waits for them, and re-layouts: none -> 47.1 us  [exchange_blocks(): received = lax.all_to_all(jnp.stack(pieces), name, 0, 0)]
    unnamed x11 -> x78, local copies, waits for them, and re-layouts: 93.9 us -> 132 us
    reshape x0 -> x2, local copies, waits for them, and re-layouts: none -> 12.3 us  [the longest x1 11.9 us: shards(): arrived.reshape(all_occ, node_count * per_peer, ao_part)]
    gather x1 -> x2, local copies, waits for them, and re-layouts: 6.39 us -> 18.3 us  [shards(): jnp.take(home_rows, block_id.reshape(-1), axis=1)]
where the time goes in v1:
time: 625 us; the launch traced here: 615 us
  waiting for transfers between devices  290 us (46%)
  local copies, waits for them, and re-layouts  218 us (35%)
  matrix products  53.9 us (9%)
  starting transfers between devices  27.8 us (4%)
  between operations  13.5 us (2%)
  other arithmetic  11.4 us (2%)
    all_to_all x1, waiting for transfers between devices, shards(): lax.all_to_all(packed, 'occ', split_axis=1, concat_axis=1, tiled=True)  181 us
    unnamed x78, local copies, waits for them, and re-layouts  132 us
    another operation x69, local copies, waits for them, and re-layouts, exchange_blocks(): received = lax.all_to_all(jnp.stack(pieces), name, 0, 0)  47.1 us
    unnamed x4, waiting for transfers between devices  28.8 us
    reduce_scatter x1, waiting for transfers between devices, shards(): lax.psum_scatter(partial_x.astype(jnp.bfloat16), 'ao', scatter_dimension=...  26.7 us
    reduce_scatter x1, waiting for transfers between devices, shards(): lax.psum_scatter(partial_s.astype(jnp.bfloat16), 'ao', scatter_dimension=...  19.4 us
    gather x2, local copies, waits for them, and re-layouts, shards(): jnp.take(home_rows, block_id.reshape(-1), axis=1)  18.3 us
    all_to_all x1, waiting for transfers between devices, shards(): lax.all_to_all(ladder, 'occ', split_axis=0, concat_axis=1, tiled=True)  17.5 us
  transfers between devices with their start and end apart: 6, of which 6 were waited for; matrix products, arithmetic and copies ran while one was open for 1% of the time, Pallas kernels for 0%

profile of v1, /device:TPU:8, one launch (start us, length us, event | category | flops | bytes accessed | tf_op | source)
XLA Modules:
  0.0 614.9 jit_solution(16077765263909051606)
XLA Ops:
  7.5 2.4 fusion.12
  12.5 26.7 %reduce-scatter.6.cloned.1.call-done = bf16[4,256,128]{1,2,0:T(8,128)(2,1)} async-done(((bf16[4,256,512]{1,2,0:T(8,128)(2,1)}), bf16[4,256,128]{1,2,0:T(8,128)(2,1)}) %reduce-scatter.6.cloned.1.call-update) | async-done | bytes 262160 | tf_op jit(solution)/shard_map/reduce_scatter | solution.py:25
  40.7 2.1 slice_bitcast_fusion.38
  42.8 2.2 slice_bitcast_fusion.19
  125.1 10.6 %all-to-all-start = ((bf16[64,4,8,128]{3,2,1,0:T(8,128)(2,1)}), bf16[64,4,8,128]{3,2,1,0:T(8,128)(2,1)S(1)}, u32[]{:S(2)}, u32[]{:S(2)}) async-start(bf16[64,4,8,128]{3,2,1,0:T(8,128)(2,1)} %constant_dynamic-update-slice_fusion), calls=%async_computation.1 | async-start | bytes 1048576 | tf_op jit(solution)/shard_map/all_to_all | solution.py:9
  136.5 16.7 %all-to-all-done = bf16[64,4,8,128]{3,2,1,0:T(8,128)(2,1)S(1)} async-done(((bf16[64,4,8,128]{3,2,1,0:T(8,128)(2,1)}), bf16[64,4,8,128]{3,2,1,0:T(8,128)(2,1)S(1)}, u32[]{:S(2)}, u32[]{:S(2)}) %all-to-all-start) | async-done | bytes 524320 | tf_op jit(solution)/shard_map/all_to_all | solution.py:9
  153.5 6.4 %gather_fusion = bf16[128,256,128]{1,2,0:T(8,128)(2,1)} fusion(bf16[256,8,128]{0,2,1:T(8,128)(2,1)S(1)} %copy.235, s32[1024]{0:T(1024)S(1)} %pad_clamp_fusion.1), kind=kCustom, calls=%fused_computation | custom fusion | bytes 16777728 | tf_op jit(solution)/shard_map/jit(_take)/gather | solution.py:42
  159.9 12.0 %copy.236 = bf16[256,128,128]{2,0,1:T(8,128)(2,1)} copy(bf16[256,128,128]{0,2,1:T(8,128)(2,1)} %bitcast.196) | data formatting | bytes 16777216 | tf_op jit(solution)/shard_map/jit(_take)/gather | solution.py:42
  171.9 7.4 %broadcast_select_fusion = bf16[256,64,2,128]{3,0,2,1:T(8,128)(2,1)} fusion(bf16[256,64,2,128]{3,0,2,1:T(8,128)(2,1)} %bitcast.197, pred[64,2]{1,0:T(8,128)(4,1)S(1)} %copy.168), kind=kLoop, calls=%fused_computation.7 | loop fusion | flops 4194304 | bytes 16777344 | tf_op jit(solution)/shard_map/jit(_take)/select_n | solution.py:42
  179.3 6.2 %all-to-all-start.1 = ((bf16[256,64,2,128]{3,0,2,1:T(8,128)(2,1)}), bf16[256,64,2,128]{3,0,2,1:T(8,128)(2,1)}, u32[]{:S(2)}, u32[]{:S(2)}) async-start(bf16[256,64,2,128]{3,0,2,1:T(8,128)(2,1)} %broadcast_select_fusion), calls=%async_computation.2 | async-start | bytes 16777216 | tf_op jit(solution)/shard_map/all_to_all | solution.py:45
  189.6 181.2 %all-to-all-done.1 = bf16[256,64,2,128]{3,0,2,1:T(8,128)(2,1)} async-done(((bf16[256,64,2,128]{3,0,2,1:T(8,128)(2,1)}), bf16[256,64,2,128]{3,0,2,1:T(8,128)(2,1)}, u32[]{:S(2)}, u32[]{:S(2)}) %all-to-all-start.1) | async-done | bytes 8388640 | tf_op jit(solution)/shard_map/all_to_all | solution.py:45
  370.7 11.9 %copy.237 = bf16[256,128,128]{0,2,1:T(8,128)(2,1)} copy(bf16[256,128,128]{2,0,1:T(8,128)(2,1)} %bitcast.73) | data formatting | bytes 16777216 | tf_op jit(solution)/shard_map/reshape | solution.py:51
  382.7 6.2 %gather_fusion.1 = bf16[64,256,128]{1,2,0:T(8,128)(2,1)} fusion(bf16[256,128,128]{0,2,1:T(8,128)(2,1)} %copy.237, s32[1024]{0:T(1024)S(1)} %pad_clamp_fusion), kind=kCustom, calls=%fused_computation.1 | custom fusion | bytes 8388864 | tf_op jit(solution)/shard_map/jit(_take)/gather | solution.py:50
  388.9 17.0 %subtract_convert_fusion = (bf16[64,256,512]{2,1,0:T(8,128)(2,1)}, bf16[64,256,512]{2,1,0:T(8,128)(2,1)}) fusion(bf16[64,512,128]{2,1,0:T(8,128)(2,1)} %param.9, bf16[64,256,128]{1,2,0:T(8,128)(2,1)} %gather_fusion.1, pred[64]{0:T(512)(128)(4,1)S(1)} %compare_and_fusion.1), kind=kOutput, calls=%fused_computation.2 | convolution fusion | flops 2183135232 | bytes 46137408 | tf_op jit(solution)/shard_map/itn,tsn->tis/dot_general | solution.py:62
  406.0 16.7 %fusion = f32[256,512,8]{1,2,0:T(8,128)S(1)} fusion(bf16[64,256,512]{2,1,0:T(8,128)(2,1)} %get-tuple-element.5, s32[64]{0:T(128)S(1)} %fusion.38, pred[64]{0:T(512)(128)(4,1)S(1)} %iota_compare_fusion.3), kind=kOutput, calls=%fused_computation.3 | convolution fusion | flops 134218752 | bytes 20971840 | tf_op jit(solution)/shard_map/tr,tis->irs/dot_general | solution.py:66
  422.7 15.0 %fusion.8 = bf16[256,8,512]{2,1,0:T(8,128)(2,1)S(1)} fusion(f32[256,512,8]{1,2,0:T(8,128)S(1)} %fusion, bf16[64,256,512]{2,1,0:T(8,128)(2,1)} %get-tuple-element.6, s32[64]{0:T(128)S(1)} %fusion.38, pred[64]{0:T(512)(128)(4,1)S(1)} %iota_compare_fusion.3), kind=kOutput, calls=%fused_computation.13 | convolution fusion | flops 136315904 | bytes 23068992 | tf_op jit(solution)/shard_map/tr,tis->irs/dot_general | solution.py:65
  437.7 23.9 %copy.248 = bf16[256,8,512]{1,0,2:T(8,128)(2,1)} copy(bf16[256,8,512]{2,1,0:T(8,128)(2,1)S(1)} %fusion.8) | data formatting | bytes 4194304
  461.6 48.5 %reshape.134 = bf16[512,2048]{1,0:T(8,128)(2,1)} reshape(bf16[512,256,8]{2,1,0:T(8,128)(2,1)} %bitcast.195) | data formatting | bytes 4194304
  510.1 28.7 %reduce-scatter.10.cloned.1.call-done = bf16[128,2048]{1,0:T(8,128)(2,1)} async-done(((bf16[512,2048]{1,0:T(8,128)(2,1)}), bf16[128,2048]{1,0:T(8,128)(2,1)}) %reduce-scatter.10.cloned.1.call-update) | async-done | bytes 524304
  538.8 12.1 %reshape.135 = bf16[128,256,8]{2,1,0:T(8,128)(2,1)} reshape(bf16[128,2048]{1,0:T(8,128)(2,1)} %reduce-scatter.10.cloned.1.call-done) | data formatting | bytes 1048576
  550.9 8.2 %copy.249 = bf16[256,8,128]{2,1,0:T(8,128)(2,1)} copy(bf16[256,8,128]{1,0,2:T(8,128)(2,1)} %bitcast.198) | data formatting | bytes 1048576
  559.1 10.6 %all-to-all-start.2 = ((bf16[256,8,128]{2,1,0:T(8,128)(2,1)}), bf16[256,8,128]{2,1,0:T(8,128)(2,1)S(1)}, u32[]{:S(2)}, u32[]{:S(2)}) async-start(bf16[256,8,128]{2,1,0:T(8,128)(2,1)} %copy.249), calls=%async_computation.3 | async-start | bytes 1048576 | tf_op jit(solution)/shard_map/all_to_all | solution.py:70
  569.7 17.5 %all-to-all-done.2 = bf16[256,8,128]{2,1,0:T(8,128)(2,1)S(1)} async-done(((bf16[256,8,128]{2,1,0:T(8,128)(2,1)}), bf16[256,8,128]{2,1,0:T(8,128)(2,1)S(1)}, u32[]{:S(2)}, u32[]{:S(2)}) %all-to-all-start.2) | async-done | bytes 524320 | tf_op jit(solution)/shard_map/all_to_all | solution.py:70
  588.8 19.4 %reduce-scatter.8.cloned.1.call-done = bf16[4,256,64]{1,2,0:T(8,128)(2,1)} async-done(((bf16[4,256,256]{1,2,0:T(8,128)(2,1)}), bf16[4,256,64]{1,2,0:T(8,128)(2,1)}) %reduce-scatter.8.cloned.1.call-update) | async-done | bytes 131088 | tf_op jit(solution)/shard_map/reduce_scatter | solution.py:75
  (172 shorter events, 92.0 us)
Async XLA Ops:
  6.5 1.0 copy-start
  6.5 32.6 %reduce-scatter.6.cloned.1.call-start = ((), (), s32[]{:S(2)}) async-start(), calls=%async_computation.6 | async-start | bytes 1310720 | tf_op jit(solution)/shard_map/reduce_scatter | solution.py:25
  47.0 88.9 %copy-start.2 = (s32[4096]{0:T(1024)S(1)}, s32[4096]{0:T(1024)}, u32[]{:S(2)}) copy-start(s32[4096]{0:T(1024)} %param.13) | copy-start | bytes 49156
  47.2 88.4 %copy-start.1 = (s32[64,64]{1,0:T(8,128)S(1)}, s32[64,64]{1,0:T(8,128)}, u32[]{:S(2)}) copy-start(s32[64,64]{1,0:T(8,128)} %reshape_squeeze.3) | copy-start | bytes 49156
  125.1 28.1 %all-to-all-start = ((bf16[64,4,8,128]{3,2,1,0:T(8,128)(2,1)}), bf16[64,4,8,128]{3,2,1,0:T(8,128)(2,1)S(1)}, u32[]{:S(2)}, u32[]{:S(2)}) async-start(bf16[64,4,8,128]{3,2,1,0:T(8,128)(2,1)} %constant_dynamic-update-slice_fusion), calls=%async_computation.1 | async-start | bytes 1048576 | tf_op jit(solution)/shard_map/all_to_all | solution.py:9
  179.3 6.7 %copy-start.3 = (s32[4096]{0:T(1024)S(1)}, s32[4096]{0:T(1024)}, u32[]{:S(2)}) copy-start(s32[4096]{0:T(1024)} %param.11) | copy-start | bytes 49156
  179.3 6.8 %copy-start.4 = (s32[64]{0:T(128)S(1)}, s32[64]{0:T(128)}, u32[]{:S(2)}) copy-start(s32[64]{0:T(128)} %param.10) | copy-start | bytes 772
  179.3 191.5 %all-to-all-start.1 = ((bf16[256,64,2,128]{3,0,2,1:T(8,128)(2,1)}), bf16[256,64,2,128]{3,0,2,1:T(8,128)(2,1)}, u32[]{:S(2)}, u32[]{:S(2)}) async-start(bf16[256,64,2,128]{3,0,2,1:T(8,128)(2,1)} %broadcast_select_fusion), calls=%async_computation.2 | async-start | bytes 16777216 | tf_op jit(solution)/shard_map/all_to_all | solution.py:45
  185.5 353.4 %reduce-scatter.10.cloned.1.call-start = ((), (), s32[]{:S(2)}) async-start(), calls=%async_computation.8 | async-start | bytes 2621440
  559.1 28.1 %all-to-all-start.2 = ((bf16[256,8,128]{2,1,0:T(8,128)(2,1)}), bf16[256,8,128]{2,1,0:T(8,128)(2,1)S(1)}, u32[]{:S(2)}, u32[]{:S(2)}) async-start(bf16[256,8,128]{2,1,0:T(8,128)(2,1)} %copy.249), calls=%async_computation.3 | async-start | bytes 1048576 | tf_op jit(solution)/shard_map/all_to_all | solution.py:70
  569.7 38.4 %reduce-scatter.8.cloned.1.call-start = ((), (), s32[]{:S(2)}) async-start(), calls=%async_computation.7 | async-start | bytes 655360 | tf_op jit(solution)/shard_map/reduce_scatter | solution.py:75
Sparse Core Ops, SparseCore 0:
  10.0 29.0 reduce-scatter.5
  510.2 28.5 reduce-scatter.9
  588.9 19.2 reduce-scatter.7
